TPU v7x, 32 devices: a whole 2x2x4 slice. The times are simulated.
32 devices in a mesh: aux: 4 (over z), pair: 8 (over y, x, core).
Axes of the slice: x: 2, y: 2, z: 4, core: 2. Of those that a mesh axis runs over, the one named last changes fastest.
Arguments:
- metric: bfloat16 [4096, 4096], P('aux', 'pair'), may hold values from -0.09375 to 0.09375
- amplitudes: bfloat16 [4096, 16384], P('aux', 'pair'), may hold values from -0.59765625 to 0.59765625
- virt_coef: bfloat16 [1024, 1280], replicated, may hold values from -1.5 to 1.5
Outputs:
- density: float32 [4096, 4096], P('aux', 'pair')
- fitted_ao: bfloat16 [4096, 20480], P(('aux', 'pair'))
All inputs are finite; a program needn't handle non-finite values.
Results may differ from a plain program's by a relative error of at most 0.012.
Values may be sent and summed in bfloat16 or wider, within the bound.
A program may use at most 128 MiB of HBM per device.

v0:
```python
import jax
import jax.numpy as jnp
from jax import lax
from jax.sharding import PartitionSpec as P


def shards(metric, amplitudes, virt_coef):
    rows_metric = lax.all_gather(metric, "pair", axis=1, tiled=True)
    full_amp = lax.all_gather(amplitudes, "aux", axis=0, tiled=True)
    fitted = jnp.dot(rows_metric, full_amp, preferred_element_type=jnp.float32).astype(jnp.bfloat16)
    partial_value = lax.dot_general(
        fitted, full_amp, (((1,), (1,)), ((), ())), preferred_element_type=jnp.float32
    )
    density = lax.psum_scatter(
        partial_value.astype(jnp.bfloat16), "pair", scatter_dimension=1, tiled=True
    ).astype(jnp.float32)
    regrouped = lax.all_to_all(fitted, "pair", split_axis=0, concat_axis=1, tiled=True)
    row_count = regrouped.shape[0]
    virt_count = virt_coef.shape[0]
    ao_count = virt_coef.shape[1]
    occ_count = regrouped.shape[1] // virt_count
    blocks = regrouped.reshape(row_count * occ_count, virt_count)
    fitted_ao = jnp.dot(blocks, virt_coef, preferred_element_type=jnp.float32).astype(jnp.bfloat16)
    return (density, fitted_ao.reshape(row_count, occ_count * ao_count))


def solution(mesh):
    in_specs = (P("aux", "pair"), P("aux", "pair"), P())
    out_specs = (P("aux", "pair"), P(("aux", "pair"), None))
    return jax.shard_map(shards, mesh=mesh, in_specs=in_specs, out_specs=out_specs, check_vma=False)
```

profile of v0, /device:TPU:0, one launch (start us, length us, event | category | flops | bytes accessed | tf_op | source)
XLA Modules:
  0.0 516.1 jit_solution(2569435131899505442)
XLA Ops:
  7.2 0.0 copy-start
  7.2 0.0 all-gather.3.cloned.1.call-start
  7.2 0.7 all-gather.3.cloned.1.call-update
  7.9 0.0 all-gather.5.cloned.1.call-start
  8.0 0.7 all-gather.5.cloned.1.call-update
  8.7 0.0 reduce-scatter.2.cloned.1.call-start
  8.7 59.8 %all-gather.3.cloned.1.call-done = bf16[1024,4096]{1,0:T(8,128)(2,1)} async-done(((bf16[1024,512]{1,0:T(8,128)(2,1)}), bf16[1024,4096]{1,0:T(8,128)(2,1)}) %all-gather.3.cloned.1.call-update) | async-done | bytes 8388624 | tf_op jit(solution)/shard_map/all_gather | solution.py:8
  68.5 288.4 %all-gather.5.cloned.1.call-done = bf16[4096,2048]{1,0:T(8,128)(2,1)} async-done(((bf16[1024,2048]{1,0:T(8,128)(2,1)}), bf16[4096,2048]{1,0:T(8,128)(2,1)}) %all-gather.5.cloned.1.call-update) | async-done | bytes 16777232 | tf_op jit(solution)/shard_map/all_gather | solution.py:9
  356.8 0.0 copy-start.2
  356.8 22.8 %fusion.1 = bf16[1024,2048]{1,0:T(8,128)(2,1)S(1)} fusion(bf16[1024,4096]{1,0:T(8,128)(2,1)} %all-gather.3.cloned.1.call-done, bf16[4096,2048]{1,0:T(8,128)(2,1)} %all-gather.5.cloned.1.call-done), kind=kOutput, calls=%fused_computation.3 | convolution fusion | flops 17179869184 | bytes 29360128 | tf_op jit(solution)/shard_map/dot_general | solution.py:10
  379.7 0.0 copy-start.1
  379.7 2.0 copy-done.1
  381.7 0.0 copy-done.2
  381.7 19.6 %convolution_convert_fusion.1 = bf16[1024,4096]{1,0:T(8,128)(2,1)} fusion(bf16[4096,2048]{1,0:T(8,128)(2,1)S(1)} %copy-done.2, bf16[1024,2048]{1,0:T(8,128)(2,1)S(1)} %fusion.1), kind=kOutput, calls=%fused_computation.1 | convolution fusion | flops 17184063488 | bytes 29360128 | tf_op jit(solution)/shard_map/dot_general | solution.py:11
  401.2 0.0 reduce-scatter.2.cloned.1.call-update
  401.3 75.2 %all_to_all.16 = bf16[8,128,2048]{2,1,0:T(8,128)(2,1)S(1)} all-to-all(bf16[8,128,2048]{2,1,0:T(8,128)(2,1)} %bitcast.9), channel_id=1, replica_groups=mesh['aux'=4,'pair'=8] {'pair'}, dimensions={0} | all-to-all | bytes 8388608 | tf_op jit(solution)/shard_map/all_to_all | solution.py:17
  476.4 4.4 copy.6
  480.8 7.1 %reshape.14 = bf16[2048,1024]{1,0:T(8,128)(2,1)} reshape(bf16[128,8,2048]{2,1,0:T(8,128)(2,1)} %copy.6) | data formatting | bytes 8388608 | tf_op jit(solution)/shard_map/reshape | solution.py:22
  487.9 0.0 copy-done
  487.9 10.8 %convolution_convert_fusion = bf16[2048,1280]{1,0:T(8,128)(2,1)} fusion(bf16[2048,1024]{1,0:T(8,128)(2,1)} %reshape.14, bf16[1024,1280]{1,0:T(8,128)(2,1)S(1)} %copy-done), kind=kOutput, calls=%fused_computation | convolution fusion | flops 5371330560 | bytes 12058624 | tf_op jit(solution)/shard_map/dot_general | solution.py:23
  498.7 8.1 %reshape.15 = bf16[128,20480]{1,0:T(8,128)(2,1)} reshape(bf16[2048,1280]{1,0:T(8,128)(2,1)} %convolution_convert_fusion) | data formatting | bytes 10485760 | tf_op jit(solution)/shard_map/reshape | solution.py:24
  506.7 0.0 reduce-scatter.2.cloned.1.call-done
  506.7 2.8 convert_element_type.14
Async XLA Ops:
  7.2 480.7 %copy-start = (bf16[1024,1280]{1,0:T(8,128)(2,1)S(1)}, bf16[1024,1280]{1,0:T(8,128)(2,1)}, u32[]{:S(2)}) copy-start(bf16[1024,1280]{1,0:T(8,128)(2,1)} %param.5) | copy-start | bytes 7864324
  7.2 61.3 %all-gather.3.cloned.1.call-start = ((), (), s32[]{:S(2)}) async-start(), calls=%async_computation.2 | async-start | bytes 9437184 | tf_op jit(solution)/shard_map/all_gather | solution.py:8
  7.9 348.9 %all-gather.5.cloned.1.call-start = ((), (), s32[]{:S(2)}) async-start(), calls=%async_computation.3 | async-start | bytes 20971520 | tf_op jit(solution)/shard_map/all_gather | solution.py:9
  8.7 498.0 %reduce-scatter.2.cloned.1.call-start = ((), (), s32[]{:S(2)}) async-start(), calls=%async_computation.4 | async-start | bytes 9437184 | tf_op jit(solution)/shard_map/reduce_scatter | solution.py:14
  356.8 24.9 %copy-start.2 = (bf16[4096,2048]{1,0:T(8,128)(2,1)S(1)}, bf16[4096,2048]{1,0:T(8,128)(2,1)}, u32[]{:S(2)}) copy-start(bf16[4096,2048]{1,0:T(8,128)(2,1)} %all-gather.5.cloned.1.call-done) | copy-start | bytes 50331652
  379.7 2.0 copy-start.1
Sparse Core Ops, SparseCore 0:
  9.9 58.5 all-gather.2
  70.0 286.7 all-gather.4
  401.4 92.9 reduce-scatter.1
where the time goes:
time: 517 us; the launch traced here: 516 us
  waiting for transfers between devices  350 us (68%)
  blocking collectives  75.2 us (15%)
  matrix products  53.1 us (10%)
  local copies, waits for them, and re-layouts  21.5 us (4%)
  between operations  13.8 us (3%)
    all_gather x1, waiting for transfers between devices, shards(): full_amp = lax.all_gather(amplitudes, 'aux', axis=0, tiled=True)  288 us
    all_to_all x1, blocking collectives, shards(): lax.all_to_all(fitted, 'pair', split_axis=0, concat_axis=1, tiled=True)  75.2 us
    all_gather x1, waiting for transfers between devices, shards(): rows_metric = lax.all_gather(metric, 'pair', axis=1, tiled=True)  59.8 us
    dot_general x1, matrix products, shards(): jnp.dot(rows_metric, full_amp, preferred_element_type=jnp.float32)  22.8 us
    dot_general x1, matrix products, shards(): lax.dot_general(fitted, full_amp, (((1,), (1,)), ((), ())), preferred_ele...  19.6 us
    dot_general x1, matrix products, shards(): jnp.dot(blocks, virt_coef, preferred_element_type=jnp.float32)  10.8 us
  transfers between devices with their start and end apart: 3, of which 2 were waited for; matrix products, arithmetic and copies ran while one was open for 6% of the time, Pallas kernels for 0%

commit v1 on v0

--- a/solution.py
+++ b/solution.py
@@ -6,7 +6,12 @@
 
 def shards(metric, amplitudes, virt_coef):
     rows_metric = lax.all_gather(metric, "pair", axis=1, tiled=True)
-    full_amp = lax.all_gather(amplitudes, "aux", axis=0, tiled=True)
+    ring = [amplitudes]
+    for hop in range(3):
+        ring.append(lax.ppermute(ring[-1], "aux", [(dev, (dev + 1) % 4) for dev in range(4)]))
+    full_amp = jnp.roll(
+        jnp.concatenate(ring[::-1], axis=0), (lax.axis_index("aux") + 1) * ring[0].shape[0], axis=0
+    )
     fitted = jnp.dot(rows_metric, full_amp, preferred_element_type=jnp.float32).astype(jnp.bfloat16)
     partial_value = lax.dot_general(
         fitted, full_amp, (((1,), (1,)), ((), ())), preferred_element_type=jnp.float32

time: 517 us -> 486 us (0.940)
  waiting for transfers between devices: 350 us -> 280 us
  local copies, waits for them, and re-layouts: 21.5 us -> 54.6 us
    all_gather x1 -> x0, waiting for transfers between devices: 288 us -> none  [shards(): full_amp = lax.all_gather(amplitudes, 'aux', axis=0, tiled=True)]
    ppermute x0 -> x3, waiting for transfers between devices: none -> 280 us  [shards(): lax.ppermute(ring[-1], 'aux', [(dev, (dev + 1) % 4) for dev in range(4)])]
    all_gather x1, waiting for transfers between devices: 59.8 us -> 0.01 us  [shards(): rows_metric = lax.all_gather(metric, 'pair', axis=1, tiled=True)]
    unnamed x6 -> x13, local copies, waits for them, and re-layouts: 2.02 us -> 32.8 us
  transfers between devices with their start and end apart: 3 -> 5, of which waited for: 2 -> 3; matrix products, arithmetic and copies ran while one was open for 6% -> 13% of each run, Pallas kernels for 0% -> 0%
where the time goes in v1:
time: 486 us; the launch traced here: 485 us
  waiting for transfers between devices  280 us (58%)
  blocking collectives  75.1 us (15%)
  matrix products  55.2 us (11%)
  local copies, waits for them, and re-layouts  54.6 us (11%)
  between operations  14.1 us (3%)
    ppermute x3, waiting for transfers between devices, shards(): lax.ppermute(ring[-1], 'aux', [(dev, (dev + 1) % 4) for dev in range(4)])  280 us
    all_to_all x1, blocking collectives, shards(): lax.all_to_all(fitted, 'pair', split_axis=0, concat_axis=1, tiled=True)  75.1 us
    unnamed x13, local copies, waits for them, and re-layouts  32.8 us
    dot_general x1, matrix products, shards(): jnp.dot(rows_metric, full_amp, preferred_element_type=jnp.float32)  22.7 us
    dot_general x1, matrix products, shards(): lax.dot_general(fitted, full_amp, (((1,), (1,)), ((), ())), preferred_ele...  21.7 us
    dot_general x1, matrix products, shards(): jnp.dot(blocks, virt_coef, preferred_element_type=jnp.float32)  10.8 us
  transfers between devices with their start and end apart: 5, of which 3 were waited for; matrix products, arithmetic and copies ran while one was open for 13% of the time, Pallas kernels for 0%

profile of v1, /device:TPU:0, one launch (start us, length us, event | category | flops | bytes accessed | tf_op | source)
XLA Modules:
  0.0 484.7 jit_solution(10569450406399106259)
XLA Ops:
  7.2 0.0 copy-start
  7.2 0.0 all-gather.2.cloned.1.call-start
  7.2 3.1 collective-permute-start
  10.3 0.0 all-gather.2.cloned.1.call-update
  10.4 0.0 reduce-scatter.2.cloned.1.call-start
  10.4 92.8 %collective-permute-done = bf16[1024,2048]{1,0:T(8,128)(2,1)} collective-permute-done((bf16[1024,2048]{1,0:T(8,128)(2,1)}, bf16[1024,2048]{1,0:T(8,128)(2,1)}, u32[]{:S(2)}, u32[]{:S(2)}) %collective-permute-start) | collective-permute-done | bytes 4194336 | tf_op jit(solution)/shard_map/ppermute | solution.py:11
  103.2 0.0 collective-permute-start.1
  103.2 93.8 %collective-permute-done.1 = bf16[1024,2048]{1,0:T(8,128)(2,1)} collective-permute-done((bf16[1024,2048]{1,0:T(8,128)(2,1)}, bf16[1024,2048]{1,0:T(8,128)(2,1)}, u32[]{:S(2)}, u32[]{:S(2)}) %collective-permute-start.1) | collective-permute-done | bytes 4194336 | tf_op jit(solution)/shard_map/ppermute | solution.py:11
  197.1 0.0 collective-permute-start.2
  197.1 93.0 %collective-permute-done.2 = bf16[1024,2048]{1,0:T(8,128)(2,1)} collective-permute-done((bf16[1024,2048]{1,0:T(8,128)(2,1)}, bf16[1024,2048]{1,0:T(8,128)(2,1)}, u32[]{:S(2)}, u32[]{:S(2)}) %collective-permute-start.2) | collective-permute-done | bytes 4194336 | tf_op jit(solution)/shard_map/ppermute | solution.py:11
  290.1 4.7 constant_dynamic-update-slice_fusion.7
  294.8 0.0 copy-start.1
  294.8 4.9 %constant_dynamic-update-slice_fusion.6 = bf16[8192,2048]{1,0:T(8,128)(2,1)} fusion(bf16[8192,2048]{1,0:T(8,128)(2,1)} %constant_dynamic-update-slice_fusion.7, bf16[1024,2048]{1,0:T(8,128)(2,1)} %collective-permute-done.1), kind=kLoop, calls=%fused_computation.13 | loop fusion | bytes 8388608
  299.7 4.7 constant_dynamic-update-slice_fusion.5
  304.5 0.0 copy-done.1
  304.5 2.2 constant_dynamic-update-slice_fusion.4
  306.7 4.7 constant_dynamic-update-slice_fusion.3
  311.4 4.7 constant_dynamic-update-slice_fusion.2
  316.2 4.7 constant_dynamic-update-slice_fusion.1
  320.9 2.2 constant_dynamic-update-slice_fusion
  323.1 0.0 all-gather.2.cloned.1.call-done
  323.1 22.7 %fusion.2 = bf16[2048,1024]{0,1:T(8,128)(2,1)S(1)} fusion(bf16[1024,4096]{1,0:T(8,128)(2,1)} %all-gather.2.cloned.1.call-done, bf16[8192,2048]{1,0:T(8,128)(2,1)} %constant_dynamic-update-slice_fusion, s32[]{:T(128)S(6)} %select_n.14), kind=kOutput, calls=%fused_computation.2 | convolution fusion | flops 17179869184 | bytes 29360132 | tf_op jit(solution)/shard_map/dot_general | solution.py:15
  345.8 0.0 copy-start.2
  345.8 2.0 copy-done.2
  347.8 21.7 %fusion.4 = bf16[1024,4096]{1,0:T(8,128)(2,1)} fusion(bf16[8192,2048]{1,0:T(8,128)(2,1)} %constant_dynamic-update-slice_fusion, s32[]{:T(128)S(6)} %select_n.14, bf16[2048,1024]{0,1:T(8,128)(2,1)S(1)} %fusion.2), kind=kOutput, calls=%fused_computation.4 | convolution fusion | flops 17184063488 | bytes 29360132 | tf_op jit(solution)/shard_map/dot_general | solution.py:16
  369.6 0.0 reduce-scatter.2.cloned.1.call-update
  369.6 75.1 %all_to_all.16 = bf16[8,128,2048]{2,1,0:T(8,128)(2,1)S(1)} all-to-all(bf16[8,128,2048]{2,1,0:T(8,128)(2,1)} %bitcast.9), channel_id=1, replica_groups=mesh['aux'=4,'pair'=8] {'pair'}, dimensions={0} | all-to-all | bytes 8388608 | tf_op jit(solution)/shard_map/all_to_all | solution.py:22
  444.7 4.3 copy.6
  449.0 7.2 %reshape.14 = bf16[2048,1024]{1,0:T(8,128)(2,1)} reshape(bf16[128,8,2048]{2,1,0:T(8,128)(2,1)} %copy.6) | data formatting | bytes 8388608 | tf_op jit(solution)/shard_map/reshape | solution.py:27
  456.2 0.0 copy-done
  456.2 10.8 %convolution_convert_fusion = bf16[2048,1280]{1,0:T(8,128)(2,1)} fusion(bf16[2048,1024]{1,0:T(8,128)(2,1)} %reshape.14, bf16[1024,1280]{1,0:T(8,128)(2,1)S(1)} %copy-done), kind=kOutput, calls=%fused_computation.5 | convolution fusion | flops 5371330560 | bytes 12058624 | tf_op jit(solution)/shard_map/dot_general | solution.py:28
  467.0 8.1 %reshape.15 = bf16[128,20480]{1,0:T(8,128)(2,1)} reshape(bf16[2048,1280]{1,0:T(8,128)(2,1)} %convolution_convert_fusion) | data formatting | bytes 10485760 | tf_op jit(solution)/shard_map/reshape | solution.py:29
  475.1 0.0 reduce-scatter.2.cloned.1.call-done
  475.1 2.8 convert_element_type.17
Async XLA Ops:
  7.2 449.1 %copy-start = (bf16[1024,1280]{1,0:T(8,128)(2,1)S(1)}, bf16[1024,1280]{1,0:T(8,128)(2,1)}, u32[]{:S(2)}) copy-start(bf16[1024,1280]{1,0:T(8,128)(2,1)} %param.5) | copy-start | bytes 7864324
  7.2 316.0 %all-gather.2.cloned.1.call-start = ((), (), s32[]{:S(2)}) async-start(), calls=%async_computation.2 | async-start | bytes 9437184 | tf_op jit(solution)/shard_map/all_gather | solution.py:8
  7.2 96.0 %collective-permute-start = (bf16[1024,2048]{1,0:T(8,128)(2,1)}, bf16[1024,2048]{1,0:T(8,128)(2,1)}, u32[]{:S(2)}, u32[]{:S(2)}) collective-permute-start(bf16[1024,2048]{1,0:T(8,128)(2,1)} %param.4), channel_id=1, source_target_pairs={{0,8},{8,16},{16,24},{24,0},{1,9},{9,17},{17,25},{25,1},{2,10},{10... | collective-permute-start | bytes 12582920 | tf_op jit(solution)/shard_map/ppermute | solution.py:11
  10.4 464.7 %reduce-scatter.2.cloned.1.call-start = ((), (), s32[]{:S(2)}) async-start(), calls=%async_computation.3 | async-start | bytes 9437184 | tf_op jit(solution)/shard_map/reduce_scatter | solution.py:19
  103.2 93.8 %collective-permute-start.1 = (bf16[1024,2048]{1,0:T(8,128)(2,1)}, bf16[1024,2048]{1,0:T(8,128)(2,1)}, u32[]{:S(2)}, u32[]{:S(2)}) collective-permute-start(bf16[1024,2048]{1,0:T(8,128)(2,1)} %collective-permute-done), channel_id=1, source_target_pairs={{0,8},{8,16},{16,24},{24,0},{1,9},{9,17},{17,25},{25,1},{2,10},{10... | collective-permute-start | bytes 12582920 | tf_op jit(solution)/shard_map/ppermute | solution.py:11
  197.1 93.0 %collective-permute-start.2 = (bf16[1024,2048]{1,0:T(8,128)(2,1)}, bf16[1024,2048]{1,0:T(8,128)(2,1)}, u32[]{:S(2)}, u32[]{:S(2)}) collective-permute-start(bf16[1024,2048]{1,0:T(8,128)(2,1)} %collective-permute-done.1), channel_id=1, source_target_pairs={{0,8},{8,16},{16,24},{24,0},{1,9},{9,17},{17,25},{25,1},{2,10},{10... | collective-permute-start | bytes 12582920 | tf_op jit(solution)/shard_map/ppermute | solution.py:11
  294.8 9.7 %copy-start.1 = (bf16[1024,2048]{1,0:T(8,128)(2,1)S(1)}, bf16[1024,2048]{1,0:T(8,128)(2,1)}, u32[]{:S(2)}) copy-start(bf16[1024,2048]{1,0:T(8,128)(2,1)} %param.4) | copy-start | bytes 12582916
  345.8 2.0 copy-start.2
Sparse Core Ops, SparseCore 0:
  10.5 57.9 all-gather.1
  369.7 92.8 reduce-scatter.1
